TPU v7x, 256 devices: a whole 4x4x8 slice. The times are simulated.
256 devices in a mesh: period: 128 (over z, x, y), half: 2 (over core).
Axes of the slice: x: 4, y: 4, z: 8, core: 2. Of those that a mesh axis runs over, the one named last changes fastest.
Arguments:
- probes: float32 [1024, 4, 512], P('period', None, 'half'), may hold values from -6 to 6
- footprints: bfloat16 [1024, 512, 512], P('period', None, 'half'), may hold values from -0.25 to 0.25
- lag_weights: float32 [1024, 4], P('period'), may hold values from 0.2 to 2
- owners: int32 [1024, 4], P('period'), may hold values from 0 to 127, all different within a row; in each aligned block of 8 rows (0 to 7, 8 to 15, ...) at most 2 rows name the same one
- window_tiles: int32 [1024, 2], P('period', 'half'), may hold values from 0 to 10
- coords: int32 [2, 3072], replicated, may hold values from 0 to 63
- temporal: float32 [128, 128], replicated, as said below
Outputs:
- coefficients: float32 [4, 4], replicated
- residual: float32 [1024, 4, 512], P('period', None, 'half')
Inputs may be any that keep to these rules, and one draw needn't show every extreme that they name: `owners`: each row names 4 different periods. Among the 8 rows of one index of period, no period is named more than 2 times, and one is named exactly 2 times. `temporal`: symmetric.
All inputs are finite; a program needn't handle non-finite values.
Results may differ from a plain program's by a relative error of at most 0.025.
Values may be sent and summed in bfloat16 or wider, within the bound.
No kernel may reach another device: no remote copies, remote signals or barrier semaphores. Data moves between devices by JAX's collectives and lax.ppermute only.
A program may use at most 64 MiB of HBM per device.

v0:
```python
import jax
import jax.numpy as jnp
from jax import lax
from jax.sharding import PartitionSpec as P

epsilon = 1e-06
kernel_scale = 0.05
kernel_length = 6.0
highest = lax.Precision.HIGHEST


def from_partner(block, axis, bit):
    count = lax.axis_size(axis)
    route = []
    for low in range(count):
        high = low | 1 << bit
        if high != low and high < count:
            route += [(low, high), (high, low)]
    return lax.ppermute(block, axis, route)


def body(probes, footprints, lag_weights, owners, window_tiles, coords, temporal):
    periods = lax.axis_size("period")
    half_index = lax.axis_index("half")
    block_count, top_count = owners.shape
    probe_count = probes.shape[1]
    sound_count = footprints.shape[1]
    window = footprints.shape[2]
    win_tiles = window // 128
    cell_count = coords.shape[1]
    half_cells = cell_count // 2
    tile_count = half_cells // 128
    group_cells = half_cells // periods
    total_rows = float(block_count * periods * sound_count)
    tiles = window_tiles[:, 0]
    tile_hot = (
        tiles[:, None, None] + jnp.arange(win_tiles, dtype=jnp.int32)[None, :, None]
        == jnp.arange(tile_count, dtype=jnp.int32)[None, None, :]
    ).astype(jnp.float32)
    own_coords = lax.dynamic_slice_in_dim(coords, half_index * half_cells, half_cells, 1)
    delta_x = own_coords[0][:, None] - coords[0][None, :]
    delta_y = own_coords[1][:, None] - coords[1][None, :]
    squared = (delta_x * delta_x + delta_y * delta_y).astype(jnp.float32)
    kernel_rows = (kernel_scale * jnp.exp(-jnp.sqrt(squared) / kernel_length)).reshape(
        periods, group_cells, cell_count
    )
    owner_hot = (owners[:, :, None] == jnp.arange(periods, dtype=jnp.int32)[None, None, :]).astype(
        jnp.float32
    )

    def add_half(piece_rows):
        return jnp.einsum(
            "bps,bsw->bpw", piece_rows, footprints, preferred_element_type=jnp.float32
        )

    def mix_periods(grouped_part):
        mixed_part = jnp.einsum("ts,sik->tik", temporal, grouped_part, precision=highest)
        return lax.all_to_all(mixed_part, "period", split_axis=0, concat_axis=0, tiled=True)

    def apply_operator(vector):
        vector_low = vector.astype(jnp.bfloat16)
        partial_value = add_half(lax.all_gather(vector_low, "half", axis=2, tiled=True))
        terms = lag_weights[:, :, None, None] * partial_value[:, None, :, :]
        term_tiles = terms.reshape(block_count, top_count, probe_count, win_tiles, 128)
        placed = jnp.einsum("bjt,bkpjl->bkptl", tile_hot, term_tiles, precision=highest)
        dense_terms = jnp.einsum("bkn,bkptl->nptl", owner_hot, placed, precision=highest)
        summed = lax.psum_scatter(
            dense_terms.reshape(periods, probe_count, half_cells),
            "period",
            scatter_dimension=0,
            tiled=True,
        )
        flux_half = summed[0]
        other_half = from_partner(flux_half, "half", 0)
        whole_flux = jnp.where(
            half_index == 0,
            jnp.concatenate([flux_half, other_half], axis=1),
            jnp.concatenate([other_half, flux_half], axis=1),
        )
        grouped = jnp.einsum("pc,gkc->gpk", whole_flux, kernel_rows, precision=highest)
        mixed_flux = mix_periods(
            lax.all_to_all(grouped, "period", split_axis=0, concat_axis=0, tiled=True)
        )
        field_low = (
            jnp.transpose(mixed_flux, (1, 0, 2))
            .reshape(probe_count, half_cells)
            .astype(jnp.bfloat16)
        )
        field_all = lax.all_gather(field_low[None], "period", axis=0, tiled=True)
        selected = jnp.einsum(
            "bkn,npc->bkpc",
            owner_hot.astype(jnp.bfloat16),
            field_all,
            preferred_element_type=jnp.float32,
        )
        selected = selected.reshape(block_count, top_count, probe_count, tile_count, 128)
        windows = jnp.einsum("bkptl,bjt->bkpjl", selected, tile_hot, precision=highest)
        windows = windows.astype(jnp.bfloat16).reshape(block_count, top_count, probe_count, window)
        products = jnp.einsum(
            "bkpw,bsw->bkps", windows, footprints, preferred_element_type=jnp.float32
        )
        sounded = jnp.einsum("bk,bkps->bps", lag_weights, products, precision=highest)
        return lax.psum_scatter(
            sounded.astype(jnp.bfloat16), "half", scatter_dimension=2, tiled=True
        ).astype(jnp.float32)

    def local_mean(values):
        return jnp.sum(values, axis=(0, 2))

    def lanczos_step(current, image):
        inner_sum = lax.psum(local_mean(current * image), ("period", "half"))
        alpha = inner_sum / total_rows
        remainder = image - alpha[None, :, None] * current
        square_sum = lax.psum(local_mean(remainder * remainder), ("period", "half"))
        beta = jnp.sqrt(square_sum / total_rows + epsilon)
        return (alpha, remainder, beta)

    start_sum = lax.psum(local_mean(probes * probes), ("period", "half"))
    first_q = probes / jnp.sqrt(start_sum / total_rows + epsilon)[None, :, None]
    image_one = apply_operator(first_q)
    alpha_one, rest_one, beta_one = lanczos_step(first_q, image_one)
    second_q = rest_one / beta_one[None, :, None]
    image_two = apply_operator(second_q) - beta_one[None, :, None] * first_q
    alpha_two, residual, beta_two = lanczos_step(second_q, image_two)
    coefficients = jnp.stack([alpha_one, beta_one, alpha_two, beta_two], axis=0)
    return (coefficients, residual)


def solution(mesh):
    in_specs = (
        P("period", None, "half"),
        P("period", None, "half"),
        P("period", None),
        P("period", None),
        P("period", "half"),
        P(),
        P(),
    )
    out_specs = (P(), P("period", None, "half"))
    return jax.shard_map(body, mesh=mesh, in_specs=in_specs, out_specs=out_specs, check_vma=False)
```

profile of v0, /device:TPU:1, one launch (start us, length us, event | category | flops | bytes accessed | tf_op | source)
XLA Modules:
  0.0 1305.8 jit_solution(13119377155676004425)
XLA Ops:
  7.2 1.0 multiply_reduce_fusion.3
  8.3 81.4 %psum.35 = f32[4]{0:T(128)S(1)} all-reduce(f32[4]{0:T(128)S(1)} %multiply_reduce_fusion.3), channel_id=1, replica_groups=mesh['period'=128,'half'=2] {'period','half'}, use_global_device_ids=true, to_apply=%region_1.0 | all-reduce | flops 4 | bytes 32 | tf_op jit(solution)/shard_map/psum | solution.py:118
  89.7 0.7 iota_add_fusion
  90.4 0.8 copy.24
  91.2 0.8 fusion.101
  92.0 2.5 all_gather.12
  94.5 0.4 fusion.103
  94.9 0.8 convolution_bitcast_fusion.1
  95.7 4.4 fusion.38
  100.1 5.1 copy.26
  105.3 0.6 copy-done.5
  105.9 0.6 dynamic-slice
  106.4 221.5 %all-reduce.5.cloned.1.call-done = f32[128,4,1536]{2,1,0:T(4,128)} async-done(((f32[128,4,1536]{2,1,0:T(4,128)}), f32[128,4,1536]{2,1,0:T(4,128)}) %all-reduce.5.cloned.1.call-update) | async-done | bytes 3145744
  328.0 1.4 dynamic-slice_bitcast_fusion.1
  329.4 4.9 collective-permute-start
  334.8 0.4 collective-permute-done
  335.2 46.6 %fusion.32 = f32[128,4,12]{0,1,2:T(4,128)S(1)} fusion(s32[3072]{0:T(1024)S(1)} %bitcast.132, s32[128,12]{0,1:T(8,128)S(1)} %copy.23, s32[3072]{0:T(1024)S(1)} %bitcast.130, s32[128,12]{0,1:T(8,128)S(1)} %copy.22, f32[4,1536]{1,0:T(4,128)S(1)} %collective-permute-done, f32[4,1536]{1,0:T(4,128)S(1)} %dynamic-slice_bitcast_fusion.1, pred[]{:T(512)S(6)} %eq.36), kind=kOutput, calls=%fused_computation.35 | convolution fusion | flops 268996608 | bytes 110593 | tf_op jit(solution)/shard_map/pc,gkc->gpk/dot_general | solution.py:80
  382.0 23.7 %all_to_all.20 = f32[128,4,12]{2,1,0:T(4,128)S(1)} all-to-all(f32[128,4,12]{2,1,0:T(4,128)S(1)} %copy.27), channel_id=1, replica_groups=mesh['period'=128,'half'=2] {'period'}, dimensions={0} | all-to-all | bytes 49152 | tf_op jit(solution)/shard_map/all_to_all | solution.py:82
  405.7 0.5 convolution_bitcast_fusion.3
  406.4 17.2 %all_to_all.21 = bf16[128,4,12]{2,1,0:T(4,128)(2,1)S(1)} all-to-all(bf16[128,4,12]{2,1,0:T(4,128)(2,1)S(1)} %copy.29), channel_id=1, replica_groups=mesh['period'=128,'half'=2] {'period'}, dimensions={0} | all-to-all | bytes 24576 | tf_op jit(solution)/shard_map/all_to_all | solution.py:58
  423.7 0.8 convert_element_type.80
  424.5 0.2 reduce-scatter.7.cloned.1.call-start
  424.8 94.2 %all-gather.3.cloned.1.call-done = bf16[128,4,1536]{2,1,0:T(4,128)(2,1)} async-done(((bf16[1,4,1536]{2,1,0:T(4,128)(2,1)}), bf16[128,4,1536]{2,1,0:T(4,128)(2,1)}) %all-gather.3.cloned.1.call-update) | async-done | bytes 1572880 | tf_op jit(solution)/shard_map/all_gather | solution.py:89
  519.0 2.0 fusion.24
  521.1 0.5 fusion.30
  521.7 0.6 fusion.16
  522.3 0.6 fusion.42
  523.0 0.7 copy.52
  523.7 1.3 reshape.130
  525.1 16.9 %reduce-scatter.7.cloned.1.call-done = bf16[256,32]{1,0:T(8,128)(2,1)} async-done(((bf16[512,32]{1,0:T(8,128)(2,1)}), bf16[256,32]{1,0:T(8,128)(2,1)}) %reduce-scatter.7.cloned.1.call-update) | async-done | bytes 16400
  542.0 1.2 reshape.131
  543.2 0.4 copy.53
  543.7 77.4 %psum.36 = f32[4]{0:T(128)S(1)} all-reduce(f32[4]{0:T(128)S(1)} %fusion.68), channel_id=1, replica_groups=mesh['period'=128,'half'=2] {'period','half'}, use_global_device_ids=true, to_apply=%region_5.6 | all-reduce | flops 4 | bytes 32 | tf_op jit(solution)/shard_map/psum | solution.py:111
  621.1 0.2 multiply_reduce_fusion.2
  621.3 73.1 %psum.37 = f32[4]{0:T(128)S(1)} all-reduce(f32[4]{0:T(128)S(1)} %multiply_reduce_fusion.2), channel_id=1, replica_groups=mesh['period'=128,'half'=2] {'period','half'}, use_global_device_ids=true, to_apply=%region_7.8 | all-reduce | flops 4 | bytes 32 | tf_op jit(solution)/shard_map/psum | solution.py:114
  694.5 2.2 all_gather.14
  696.7 0.4 fusion.104
  697.1 0.8 convolution_bitcast_fusion
  697.9 4.4 fusion.36
  702.3 5.1 copy.34
  707.5 223.8 %all-reduce.7.cloned.1.call-done = f32[128,4,1536]{2,1,0:T(4,128)} async-done(((f32[128,4,1536]{2,1,0:T(4,128)}), f32[128,4,1536]{2,1,0:T(4,128)}) %all-reduce.7.cloned.1.call-update) | async-done | bytes 3145744
  931.3 1.4 dynamic-slice_bitcast_fusion
  932.7 4.9 collective-permute-start.1
  937.6 0.8 collective-permute-done.1
  938.5 46.6 %fusion.33 = f32[128,4,12]{0,1,2:T(4,128)S(1)} fusion(s32[3072]{0:T(1024)S(1)} %bitcast.133, s32[128,12]{0,1:T(8,128)S(1)} %copy.23, s32[3072]{0:T(1024)S(1)} %bitcast.131, s32[128,12]{0,1:T(8,128)S(1)} %copy.22, f32[4,1536]{1,0:T(4,128)S(1)} %collective-permute-done.1, f32[4,1536]{1,0:T(4,128)S(1)} %dynamic-slice_bitcast_fusion, pred[]{:T(512)S(6)} %eq.36), kind=kOutput, calls=%fused_computation.36 | convolution fusion | flops 268996608 | bytes 110593 | tf_op jit(solution)/shard_map/pc,gkc->gpk/dot_general | solution.py:80
  985.3 23.7 %all_to_all.22 = f32[128,4,12]{2,1,0:T(4,128)S(1)} all-to-all(f32[128,4,12]{2,1,0:T(4,128)S(1)} %copy.35), channel_id=1, replica_groups=mesh['period'=128,'half'=2] {'period'}, dimensions={0} | all-to-all | bytes 49152 | tf_op jit(solution)/shard_map/all_to_all | solution.py:82
  1009.0 0.5 convolution_bitcast_fusion.2
  1009.7 17.2 %all_to_all.23 = bf16[128,4,12]{2,1,0:T(4,128)(2,1)S(1)} all-to-all(bf16[128,4,12]{2,1,0:T(4,128)(2,1)S(1)} %copy.37), channel_id=1, replica_groups=mesh['period'=128,'half'=2] {'period'}, dimensions={0} | all-to-all | bytes 24576 | tf_op jit(solution)/shard_map/all_to_all | solution.py:58
  1027.0 0.8 convert_element_type.88
  1027.9 94.5 %all-gather.5.cloned.1.call-done = bf16[128,4,1536]{2,1,0:T(4,128)(2,1)} async-done(((bf16[1,4,1536]{2,1,0:T(4,128)(2,1)}), bf16[128,4,1536]{2,1,0:T(4,128)(2,1)}) %all-gather.5.cloned.1.call-update) | async-done | bytes 1572880 | tf_op jit(solution)/shard_map/all_gather | solution.py:89
  1122.3 2.0 fusion.27
  1124.4 0.5 fusion.31
  1125.0 0.6 fusion.14
  1125.6 0.6 fusion.40
  1126.3 0.7 copy.54
  1127.0 1.3 reshape.132
  1128.4 16.9 %reduce-scatter.9.cloned.1.call-done = bf16[256,32]{1,0:T(8,128)(2,1)} async-done(((bf16[512,32]{1,0:T(8,128)(2,1)}), bf16[256,32]{1,0:T(8,128)(2,1)}) %reduce-scatter.9.cloned.1.call-update) | async-done | bytes 16400
  1145.3 1.2 reshape.133
  1146.5 0.4 copy.55
  1146.8 0.2 multiply_reduce_fusion.1
  1147.0 77.4 %psum.38 = f32[4]{0:T(128)S(1)} all-reduce(f32[4]{0:T(128)S(1)} %multiply_reduce_fusion.1), channel_id=1, replica_groups=mesh['period'=128,'half'=2] {'period','half'}, use_global_device_ids=true, to_apply=%region_11.12 | all-reduce | flops 4 | bytes 32 | tf_op jit(solution)/shard_map/psum | solution.py:111
  1224.5 0.8 multiply_reduce_fusion
  1225.3 73.1 %psum.39 = f32[4]{0:T(128)S(1)} all-reduce(f32[4]{0:T(128)S(1)} %get-tuple-element.4), channel_id=1, replica_groups=mesh['period'=128,'half'=2] {'period','half'}, use_global_device_ids=true, to_apply=%region_13.14 | all-reduce | flops 4 | bytes 32 | tf_op jit(solution)/shard_map/psum | solution.py:114
  1298.4 0.6 pad_maximum_fusion
  (48 shorter events, 2.1 us)
Async XLA Ops:
  7.2 87.3 %copy-start = (bf16[8,512,256]{2,1,0:T(8,128)(2,1)S(1)}, bf16[8,512,256]{2,1,0:T(8,128)(2,1)}, u32[]{:S(2)}) copy-start(bf16[8,512,256]{2,1,0:T(8,128)(2,1)} %param.8) | copy-start | bytes 6291460
  7.2 88.5 %copy-start.3 = (s32[8,4]{0,1:T(4,128)S(1)}, s32[8,4]{0,1:T(4,128)}, u32[]{:S(2)}) copy-start(s32[8,4]{0,1:T(4,128)} %param.10) | copy-start | bytes 388
  7.2 320.8 %all-reduce.5.cloned.1.call-start = ((), (), s32[]{:S(2)}) async-start(), calls=%async_computation.10 | async-start | bytes 6291456
  105.2 0.7 copy-start.5
  105.2 229.1 %copy-start.2 = (s32[2,3072]{1,0:T(2,128)S(1)}, s32[2,3072]{1,0:T(2,128)}, u32[]{:S(2)}) copy-start(s32[2,3072]{1,0:T(2,128)} %param.12) | copy-start | bytes 73732
  105.2 413.8 %all-gather.3.cloned.1.call-start = ((), (), s32[]{:S(2)}) async-start(), calls=%async_computation.6 | async-start | bytes 1585152 | tf_op jit(solution)/shard_map/all_gather | solution.py:89
  329.4 5.8 collective-permute-start
  335.2 70.5 %copy-start.1 = (f32[128,128]{1,0:T(8,128)S(1)}, f32[128,128]{1,0:T(8,128)}, u32[]{:S(2)}) copy-start(f32[128,128]{1,0:T(8,128)} %param.13) | copy-start | bytes 196612
  335.2 89.6 %copy-start.4 = (f32[8,4]{0,1:T(4,128)S(1)}, f32[8,4]{0,1:T(4,128)}, u32[]{:S(2)}) copy-start(f32[8,4]{0,1:T(4,128)} %param.9) | copy-start | bytes 388
  424.5 117.5 %reduce-scatter.7.cloned.1.call-start = ((), (), s32[]{:S(2)}) async-start(), calls=%async_computation.8 | async-start | bytes 196608
  525.0 406.2 %all-reduce.7.cloned.1.call-start = ((), (), s32[]{:S(2)}) async-start(), calls=%async_computation.11 | async-start | bytes 6291456
  707.4 414.9 %all-gather.5.cloned.1.call-start = ((), (), s32[]{:S(2)}) async-start(), calls=%async_computation.7 | async-start | bytes 1585152 | tf_op jit(solution)/shard_map/all_gather | solution.py:89
  932.7 5.8 collective-permute-start.1
  1027.8 117.5 %reduce-scatter.9.cloned.1.call-start = ((), (), s32[]{:S(2)}) async-start(), calls=%async_computation.9 | async-start | bytes 196608
Sparse Core Ops, SparseCore 0:
  105.3 222.5 all-reduce.4
  424.6 94.3 all-gather.2
  525.2 16.7 reduce-scatter.6
  707.5 223.6 all-reduce.6
  1027.9 94.3 all-gather.4
  1128.5 16.7 reduce-scatter.8
where the time goes:
time: 1310 us
  waiting for transfers between devices  669 us (51%)
  blocking collectives  469 us (36%)
  matrix products  113 us (9%)
  local copies, waits for them, and re-layouts  25.2 us (2%)
  between operations  14.4 us (1%)
    unnamed x10, waiting for transfers between devices  479 us
    all_gather x2, waiting for transfers between devices, apply_operator(): field_all = lax.all_gather(field_low[None], 'period', axis=0, tiled=True)  189 us
    psum x2, blocking collectives, lanczos_step(): inner_sum = lax.psum(local_mean(current * image), ('period', 'half'))  155 us
    psum x2, blocking collectives, lanczos_step(): square_sum = lax.psum(local_mean(remainder * remainder), ('period', 'half'))  146 us
    dot_general x2, matrix products, apply_operator(): jnp.einsum('pc,gkc->gpk', whole_flux, kernel_rows, precision=highest)  93.3 us
    psum x1, blocking collectives, body(): start_sum = lax.psum(local_mean(probes * probes), ('period', 'half'))  81.4 us
    all_to_all x2, blocking collectives, apply_operator(): lax.all_to_all(grouped, 'period', split_axis=0, concat_axis=0, tiled=True)  47.4 us
    all_to_all x2, blocking collectives, mix_periods(): lax.all_to_all(mixed_part, 'period', split_axis=0, concat_axis=0, tiled=T...  34.5 us
  transfers between devices with their start and end apart: 8, of which 8 were waited for; matrix products, arithmetic and copies ran while one was open for 0% of the time, Pallas kernels for 0%

commit v1 on v0

--- a/solution.py
+++ b/solution.py
@@ -86,7 +86,9 @@
             .reshape(probe_count, half_cells)
             .astype(jnp.bfloat16)
         )
-        field_all = lax.all_gather(field_low[None], "period", axis=0, tiled=True)
+        block_2 = field_low[None]
+        stack = jnp.stack([block_2] * lax.axis_size("period"))
+        field_all = jnp.concatenate(lax.all_to_all(stack, "period", 0, 0), axis=0)
         selected = jnp.einsum(
             "bkn,npc->bkpc",
             owner_hot.astype(jnp.bfloat16),

time: 1310 us -> 1210 us (0.924)
  waiting for transfers between devices: 669 us -> 509 us
  blocking collectives: 469 us -> 512 us
    all_gather x2 -> x0, waiting for transfers between devices: 189 us -> none  [apply_operator(): field_all = lax.all_gather(field_low[None], 'period', axis=0, tiled=True)]
    all_to_all x0 -> x1, blocking collectives: none -> 43.1 us  [apply_operator(): field_all = jnp.concatenate(lax.all_to_all(stack, 'period', 0, 0), axis=0)]
    all_to_all x0 -> x1, waiting for transfers between devices: none -> 36.4 us  [apply_operator(): field_all = jnp.concatenate(lax.all_to_all(stack, 'period', 0, 0), axis=0)]
    unnamed x10 -> x8, waiting for transfers between devices: 479 us -> 471 us
  transfers between devices with their start and end apart: 8 -> 7, of which waited for: 8 -> 7; matrix products, arithmetic and copies ran while one was open for 0% -> 0% of each run, Pallas kernels for 0% -> 0%
where the time goes in v1:
time: 1210 us; the launch traced here: 1200 us
  blocking collectives  512 us (42%)
  waiting for transfers between devices  509 us (42%)
  matrix products  113 us (9%)
  local copies, waits for them, and re-layouts  33.8 us (3%)
  starting transfers between devices  17.7 us (1%)
  between operations  14.4 us (1%)
    unnamed x8, waiting for transfers between devices  471 us
    psum x2, blocking collectives, lanczos_step(): inner_sum = lax.psum(local_mean(current * image), ('period', 'half'))  155 us
    psum x2, blocking collectives, lanczos_step(): square_sum = lax.psum(local_mean(remainder * remainder), ('period', 'half'))  146 us
    dot_general x2, matrix products, apply_operator(): jnp.einsum('pc,gkc->gpk', whole_flux, kernel_rows, precision=highest)  93.3 us
    psum x1, blocking collectives, body(): start_sum = lax.psum(local_mean(probes * probes), ('period', 'half'))  81.4 us
    all_to_all x2, blocking collectives, apply_operator(): lax.all_to_all(grouped, 'period', split_axis=0, concat_axis=0, tiled=True)  47.4 us
    all_to_all x1, blocking collectives, apply_operator(): field_all = jnp.concatenate(lax.all_to_all(stack, 'period', 0, 0), axis=0)  43.1 us
    all_to_all x1, waiting for transfers between devices, apply_operator(): field_all = jnp.concatenate(lax.all_to_all(stack, 'period', 0, 0), axis=0)  36.4 us
  transfers between devices with their start and end apart: 7, of which 7 were waited for; matrix products, arithmetic and copies ran while one was open for 0% of the time, Pallas kernels for 0%

profile of v1, /device:TPU:1, one launch (start us, length us, event | category | flops | bytes accessed | tf_op | source)
XLA Modules:
  0.0 1204.6 jit_solution(6609845341051771960)
XLA Ops:
  7.2 1.0 multiply_reduce_fusion.3
  8.3 81.4 %psum.35 = f32[4]{0:T(128)S(1)} all-reduce(f32[4]{0:T(128)S(1)} %multiply_reduce_fusion.3), channel_id=1, replica_groups=mesh['period'=128,'half'=2] {'period','half'}, use_global_device_ids=true, to_apply=%region_1.0 | all-reduce | flops 4 | bytes 32 | tf_op jit(solution)/shard_map/psum | solution.py:120
  89.7 0.7 iota_add_fusion
  90.4 0.8 copy.18
  91.1 0.8 fusion.91
  92.0 2.5 all_gather.6
  94.5 0.4 fusion.93
  94.9 0.8 convolution_bitcast_fusion.1
  95.7 4.4 fusion.26
  100.1 5.1 copy.20
  105.2 0.6 copy-done.5
  105.8 0.6 dynamic-slice
  106.4 221.5 %all-reduce.5.cloned.1.call-done = f32[128,4,1536]{2,1,0:T(4,128)} async-done(((f32[128,4,1536]{2,1,0:T(4,128)}), f32[128,4,1536]{2,1,0:T(4,128)}) %all-reduce.5.cloned.1.call-update) | async-done | bytes 3145744
  327.9 1.4 dynamic-slice_bitcast_fusion.1
  329.3 4.9 collective-permute-start
  334.7 0.4 collective-permute-done
  335.1 46.6 %fusion.20 = f32[128,4,12]{0,1,2:T(4,128)S(1)} fusion(s32[3072]{0:T(1024)S(1)} %bitcast.136, s32[128,12]{0,1:T(8,128)S(1)} %copy.17, s32[3072]{0:T(1024)S(1)} %bitcast.134, s32[128,12]{0,1:T(8,128)S(1)} %copy.16, f32[4,1536]{1,0:T(4,128)S(1)} %collective-permute-done, f32[4,1536]{1,0:T(4,128)S(1)} %dynamic-slice_bitcast_fusion.1, pred[]{:T(512)S(6)} %eq.36), kind=kOutput, calls=%fused_computation.27 | convolution fusion | flops 268996608 | bytes 110593 | tf_op jit(solution)/shard_map/pc,gkc->gpk/dot_general | solution.py:80
  381.9 23.7 %all_to_all.30 = f32[128,4,12]{2,1,0:T(4,128)S(1)} all-to-all(f32[128,4,12]{2,1,0:T(4,128)S(1)} %copy.21), channel_id=1, replica_groups=mesh['period'=128,'half'=2] {'period'}, dimensions={0} | all-to-all | bytes 49152 | tf_op jit(solution)/shard_map/all_to_all | solution.py:82
  405.6 0.5 convolution_bitcast_fusion.3
  406.4 17.2 %all_to_all.31 = bf16[128,4,12]{2,1,0:T(4,128)(2,1)S(1)} all-to-all(bf16[128,4,12]{2,1,0:T(4,128)(2,1)S(1)} %copy.23), channel_id=1, replica_groups=mesh['period'=128,'half'=2] {'period'}, dimensions={0} | all-to-all | bytes 24576 | tf_op jit(solution)/shard_map/all_to_all | solution.py:58
  423.8 1.6 stack.21
  425.4 7.4 all-to-all-start.2
  433.0 36.4 %all-to-all-done.2 = bf16[128,1,4,1536]{3,2,1,0:T(4,128)(2,1)} async-done(((bf16[128,1,4,1536]{3,2,1,0:T(4,128)(2,1)}), bf16[128,1,4,1536]{3,2,1,0:T(4,128)(2,1)}, u32[]{:S(2)}, u32[]{:S(2)}) %all-to-all-start.2) | async-done | bytes 1572896 | tf_op jit(solution)/shard_map/all_to_all | solution.py:91
  469.4 3.9 copy.25
  473.2 2.0 fusion.70
  475.3 0.6 fusion.18
  475.9 0.6 fusion.16
  476.5 0.6 fusion.30
  477.2 0.7 copy.46
  477.9 1.3 reshape.130
  479.3 12.9 %reduce-scatter.7.cloned.1.call-done = bf16[256,32]{1,0:T(8,128)(2,1)} async-done(((bf16[512,32]{1,0:T(8,128)(2,1)}), bf16[256,32]{1,0:T(8,128)(2,1)}) %reduce-scatter.7.cloned.1.call-update) | async-done | bytes 16400
  492.2 1.2 reshape.131
  493.4 0.4 copy.47
  493.9 77.4 %psum.36 = f32[4]{0:T(128)S(1)} all-reduce(f32[4]{0:T(128)S(1)} %fusion.56), channel_id=1, replica_groups=mesh['period'=128,'half'=2] {'period','half'}, use_global_device_ids=true, to_apply=%region_5.6 | all-reduce | flops 4 | bytes 32 | tf_op jit(solution)/shard_map/psum | solution.py:113
  571.5 73.1 %psum.37 = f32[4]{0:T(128)S(1)} all-reduce(f32[4]{0:T(128)S(1)} %multiply_reduce_fusion.2), channel_id=1, replica_groups=mesh['period'=128,'half'=2] {'period','half'}, use_global_device_ids=true, to_apply=%region_7.8 | all-reduce | flops 4 | bytes 32 | tf_op jit(solution)/shard_map/psum | solution.py:116
  644.8 2.2 all_gather.7
  647.0 0.4 fusion.94
  647.4 0.8 convolution_bitcast_fusion
  648.2 4.4 fusion.24
  652.6 5.1 copy.28
  657.7 223.8 %all-reduce.7.cloned.1.call-done = f32[128,4,1536]{2,1,0:T(4,128)} async-done(((f32[128,4,1536]{2,1,0:T(4,128)}), f32[128,4,1536]{2,1,0:T(4,128)}) %all-reduce.7.cloned.1.call-update) | async-done | bytes 3145744
  881.5 1.4 dynamic-slice_bitcast_fusion
  882.9 5.1 collective-permute-start.1
  888.1 0.8 collective-permute-done.1
  888.9 46.6 %fusion.21 = f32[128,4,12]{0,1,2:T(4,128)S(1)} fusion(s32[3072]{0:T(1024)S(1)} %bitcast.137, s32[128,12]{0,1:T(8,128)S(1)} %copy.17, s32[3072]{0:T(1024)S(1)} %bitcast.135, s32[128,12]{0,1:T(8,128)S(1)} %copy.16, f32[4,1536]{1,0:T(4,128)S(1)} %collective-permute-done.1, f32[4,1536]{1,0:T(4,128)S(1)} %dynamic-slice_bitcast_fusion, pred[]{:T(512)S(6)} %eq.36), kind=kOutput, calls=%fused_computation.28 | convolution fusion | flops 268996608 | bytes 110593 | tf_op jit(solution)/shard_map/pc,gkc->gpk/dot_general | solution.py:80
  935.7 23.7 %all_to_all.32 = f32[128,4,12]{2,1,0:T(4,128)S(1)} all-to-all(f32[128,4,12]{2,1,0:T(4,128)S(1)} %copy.29), channel_id=1, replica_groups=mesh['period'=128,'half'=2] {'period'}, dimensions={0} | all-to-all | bytes 49152 | tf_op jit(solution)/shard_map/all_to_all | solution.py:82
  959.4 0.5 convolution_bitcast_fusion.2
  960.2 17.2 %all_to_all.33 = bf16[128,4,12]{2,1,0:T(4,128)(2,1)S(1)} all-to-all(bf16[128,4,12]{2,1,0:T(4,128)(2,1)S(1)} %copy.31), channel_id=1, replica_groups=mesh['period'=128,'half'=2] {'period'}, dimensions={0} | all-to-all | bytes 24576 | tf_op jit(solution)/shard_map/all_to_all | solution.py:58
  977.6 0.4 stack.24
  978.0 43.1 %all_to_all.34 = bf16[128,1,4,1536]{3,2,1,0:T(4,128)(2,1)} all-to-all(bf16[128,1,4,1536]{3,2,1,0:T(4,128)(2,1)S(1)} %stack.24), channel_id=1, replica_groups=mesh['period'=128,'half'=2] {'period'}, dimensions={0} | all-to-all | bytes 3145728 | tf_op jit(solution)/shard_map/all_to_all | solution.py:91
  1021.2 3.9 copy.33
  1025.0 2.0 fusion.68
  1027.1 0.6 fusion.19
  1027.7 0.6 fusion.14
  1028.3 0.6 fusion.28
  1029.0 0.7 copy.48
  1029.7 1.3 reshape.132
  1031.1 13.0 %reduce-scatter.9.cloned.1.call-done = bf16[256,32]{1,0:T(8,128)(2,1)} async-done(((bf16[512,32]{1,0:T(8,128)(2,1)}), bf16[256,32]{1,0:T(8,128)(2,1)}) %reduce-scatter.9.cloned.1.call-update) | async-done | bytes 16400
  1044.0 1.2 reshape.133
  1045.2 0.4 copy.49
  1045.8 77.4 %psum.38 = f32[4]{0:T(128)S(1)} all-reduce(f32[4]{0:T(128)S(1)} %multiply_reduce_fusion.1), channel_id=1, replica_groups=mesh['period'=128,'half'=2] {'period','half'}, use_global_device_ids=true, to_apply=%region_11.12 | all-reduce | flops 4 | bytes 32 | tf_op jit(solution)/shard_map/psum | solution.py:113
  1123.2 0.8 multiply_reduce_fusion
  1124.0 73.1 %psum.39 = f32[4]{0:T(128)S(1)} all-reduce(f32[4]{0:T(128)S(1)} %get-tuple-element.4), channel_id=1, replica_groups=mesh['period'=128,'half'=2] {'period','half'}, use_global_device_ids=true, to_apply=%region_13.14 | all-reduce | flops 4 | bytes 32 | tf_op jit(solution)/shard_map/psum | solution.py:116
  1197.1 0.6 pad_maximum_fusion
  (49 shorter events, 2.8 us)
Async XLA Ops:
  7.2 87.3 %copy-start = (bf16[8,512,256]{2,1,0:T(8,128)(2,1)S(1)}, bf16[8,512,256]{2,1,0:T(8,128)(2,1)}, u32[]{:S(2)}) copy-start(bf16[8,512,256]{2,1,0:T(8,128)(2,1)} %param.8) | copy-start | bytes 6291460
  7.2 88.5 %copy-start.3 = (s32[8,4]{0,1:T(4,128)S(1)}, s32[8,4]{0,1:T(4,128)}, u32[]{:S(2)}) copy-start(s32[8,4]{0,1:T(4,128)} %param.10) | copy-start | bytes 388
  7.2 320.7 %all-reduce.5.cloned.1.call-start = ((), (), s32[]{:S(2)}) async-start(), calls=%async_computation.10 | async-start | bytes 6291456
  105.2 0.7 copy-start.5
  105.2 229.1 %copy-start.2 = (s32[2,3072]{1,0:T(2,128)S(1)}, s32[2,3072]{1,0:T(2,128)}, u32[]{:S(2)}) copy-start(s32[2,3072]{1,0:T(2,128)} %param.12) | copy-start | bytes 73732
  329.3 5.8 collective-permute-start
  335.1 70.5 %copy-start.1 = (f32[128,128]{1,0:T(8,128)S(1)}, f32[128,128]{1,0:T(8,128)}, u32[]{:S(2)}) copy-start(f32[128,128]{1,0:T(8,128)} %param.13) | copy-start | bytes 196612
  381.9 50.9 %copy-start.4 = (f32[8,4]{0,1:T(4,128)S(1)}, f32[8,4]{0,1:T(4,128)}, u32[]{:S(2)}) copy-start(f32[8,4]{0,1:T(4,128)} %param.9) | copy-start | bytes 388
  425.4 44.0 %all-to-all-start.2 = ((bf16[128,1,4,1536]{3,2,1,0:T(4,128)(2,1)}), bf16[128,1,4,1536]{3,2,1,0:T(4,128)(2,1)}, u32[]{:S(2)}, u32[]{:S(2)}) async-start(bf16[128,1,4,1536]{3,2,1,0:T(4,128)(2,1)} %stack.21), calls=%async_computation.2 | async-start | bytes 3145728 | tf_op jit(solution)/shard_map/all_to_all | solution.py:91
  432.8 59.4 %reduce-scatter.7.cloned.1.call-start = ((), (), s32[]{:S(2)}) async-start(), calls=%async_computation.8 | async-start | bytes 196608
  479.3 402.3 %all-reduce.7.cloned.1.call-start = ((), (), s32[]{:S(2)}) async-start(), calls=%async_computation.11 | async-start | bytes 6291456
  657.7 386.4 %reduce-scatter.9.cloned.1.call-start = ((), (), s32[]{:S(2)}) async-start(), calls=%async_computation.9 | async-start | bytes 196608
  882.9 6.0 collective-permute-start.1
Sparse Core Ops, SparseCore 0:
  105.3 222.5 all-reduce.4
  479.4 12.7 reduce-scatter.6
  657.8 223.6 all-reduce.6
  1031.2 12.7 reduce-scatter.8
